TPU v7x, 32 devices: a whole 2x2x4 slice. The times are simulated.
32 devices in a mesh: gx: 8 (over y, x, core), gy: 4 (over z).
Axes of the slice: x: 2, y: 2, z: 4, core: 2. Of those that a mesh axis runs over, the one named last changes fastest.
Arguments:
- probe_signs: int32 [32, 16, 64, 128], P(None, 'gx', 'gy'), may hold values from 0 to 1
- diagonal: float32 [16, 64, 128], P('gx', 'gy'), may hold values from 0.25 to 4
Outputs:
- diagonal_blocks: float32 [3, 32, 32], replicated
- offdiag_blocks: float32 [3, 32, 32], replicated
- next_block: float32 [32, 16, 64, 128], P(None, 'gx', 'gy')
All inputs are finite; a program needn't handle non-finite values.
Results may differ from a plain program's by a relative error of at most 0.0006.
Values sent between devices are 32-bit elements; how exact they have to be, the bound alone decides.
A program may use at most 64 MiB of HBM per device.

v0:
```python
import jax
import jax.numpy as jnp
from jax import lax
from jax.sharding import PartitionSpec as P

ITERS = 3


def with_halo(block, sides, width):
    for axis, dim in sides:
        count = lax.axis_size(axis)
        forward = [(i, i + 1) for i in range(count - 1)]
        forward.append((count - 1, 0))
        backward = [(target, source) for source, target in forward]
        low = lax.ppermute(
            lax.slice_in_dim(block, block.shape[dim] - width, None, axis=dim), axis, forward
        )
        high = lax.ppermute(lax.slice_in_dim(block, 0, width, axis=dim), axis, backward)
        block = jnp.concatenate([low, block, high], axis=dim)
    return block


def stencil(vectors, diagonal):
    padded = with_halo(vectors, (("gx", 1), ("gy", 2)), 1)
    beside = padded[:, 2:, 1:-1] + padded[:, :-2, 1:-1] + padded[:, 1:-1, 2:] + padded[:, 1:-1, :-2]
    beside = beside + jnp.roll(vectors, 1, 3) + jnp.roll(vectors, -1, 3)
    return (6.0 + diagonal)[None] * vectors - beside


def inner_block(left, right):
    return jnp.einsum("pxyz,qxyz->pq", left, right, precision=lax.Precision.HIGHEST)


def combine(vectors, matrix):
    return jnp.einsum("pxyz,pq->qxyz", vectors, matrix, precision=lax.Precision.HIGHEST)


def small_product(left, right):
    return jnp.dot(left, right, precision=lax.Precision.HIGHEST)


def inverse_lower(gram_matrix):
    lower_factor = jnp.linalg.cholesky(gram_matrix)
    identity_matrix = jnp.eye(gram_matrix.shape[0], dtype=gram_matrix.dtype)
    inverse = lax.linalg.triangular_solve(lower_factor, identity_matrix, left_side=True, lower=True)
    return (lower_factor, inverse)


def per_device(probe_signs, diagonal):
    total_cells = (
        probe_signs.shape[1]
        * lax.axis_size("gx")
        * probe_signs.shape[2]
        * lax.axis_size("gy")
        * probe_signs.shape[3]
    )
    scale_factor = 1.0 / jnp.sqrt(jnp.float32(total_cells))
    probes = (2.0 * probe_signs.astype(jnp.float32) - 1.0) * scale_factor
    probe_matrix = lax.psum(inner_block(probes, probes), ("gx", "gy"))
    lower_factor, inverse = inverse_lower(probe_matrix)
    current = combine(probes, inverse.T)
    previous = None
    coupling = None
    alphas = []
    betas = []
    for iteration in range(ITERS):
        image = stencil(current, diagonal)
        if previous is not None:
            image = image - combine(previous, coupling)
        projected, image_gram = lax.psum(
            (inner_block(current, image), inner_block(image, image)), ("gx", "gy")
        )
        remain = image - combine(current, projected)
        remain_gram = image_gram - small_product(projected.T, projected)
        lower_factor, inverse = inverse_lower(remain_gram)
        alphas.append(projected)
        betas.append(lower_factor.T)
        previous = current
        coupling = lower_factor
        current = combine(remain, inverse.T)
    return (jnp.stack(alphas), jnp.stack(betas), current)


def solution(mesh):
    in_specs = (P(None, "gx", "gy", None), P("gx", "gy", None))
    out_specs = (P(), P(), P(None, "gx", "gy", None))
    return jax.shard_map(
        per_device, mesh=mesh, in_specs=in_specs, out_specs=out_specs, check_vma=False
    )
```

profile of v0, /device:TPU:0, one launch (start us, length us, event | category | flops | bytes accessed | tf_op | source)
XLA Modules:
  0.0 253.0 jit_solution(12887706050572880338)
XLA Ops:
  0.6 1.1 add_multiply_fusion
  1.8 0.8 convolution_bitcast_fusion.10
  2.6 42.1 %psum.49 = f32[32,32]{0,1:T(8,128)S(1)} all-reduce(f32[32,32]{0,1:T(8,128)S(1)} %convolution_bitcast_fusion.10), channel_id=1, replica_groups=mesh['gx'=8,'gy'=4] {'gx','gy'}, use_global_device_ids=true, to_apply=%region_0.0 | all-reduce | flops 1024 | bytes 8192 | tf_op jit(solution)/shard_map/psum | solution.py:59
  44.7 2.9 %cholesky.74 = f32[32,32]{1,0:T(8,128)S(1)} custom-call(f32[32,32]{1,0:T(8,128)S(1)} %fusion.38), custom_call_target="Cholesky" | custom-call | tf_op jit(solution)/shard_map/jit(cholesky)/cholesky | solution.py:43
  47.7 0.6 compare_reduce_fusion.3
  48.3 0.7 fusion.25
  49.0 2.4 custom-call.8
  51.7 0.9 fusion.18
  52.7 2.6 %collective-permute-start = (f32[32,1,16,128]{3,0,2,1:T(8,128)S(1)}, f32[32,1,16,128]{3,0,2,1:T(8,128)S(1)}, u32[]{:S(2)}, u32[]{:S(2)}) collective-permute-start(f32[32,1,16,128]{3,0,2,1:T(8,128)S(1)} %get-tuple-element.37), channel_id=1, source_target_pairs={{4,0},{8,4},{12,8},{16,12},{20,16},{24,20},{28,24},{0,28},{5,1},{9... | collective-permute-start | bytes 786440 | tf_op jit(solution)/shard_map/ppermute | solution.py:18
  55.7 4.8 %collective-permute-done.1 = f32[32,1,16,128]{3,0,2,1:T(8,128)S(1)} collective-permute-done((f32[32,1,16,128]{3,0,2,1:T(8,128)S(1)}, f32[32,1,16,128]{3,0,2,1:T(8,128)S(1)}, u32[]{:S(2)}, u32[]{:S(2)}) %collective-permute-start.1) | collective-permute-done | bytes 262176 | tf_op jit(solution)/shard_map/ppermute | solution.py:15
  61.1 2.3 collective-permute-start.2
  63.3 2.0 collective-permute-done.2
  65.4 4.2 %collective-permute-done.3 = f32[32,4,1,128]{3,0,2,1:T(8,128)S(1)} collective-permute-done((f32[32,4,1,128]{3,0,2,1:T(8,128)S(1)}, f32[32,4,1,128]{3,0,2,1:T(8,128)S(1)}, u32[]{:S(2)}, u32[]{:S(2)}) %collective-permute-start.3) | collective-permute-done | bytes 65568 | tf_op jit(solution)/shard_map/ppermute | solution.py:15
  71.1 37.8 %all-reduce.2 = (f32[32,32]{0,1:T(8,128)S(1)}, f32[32,32]{1,0:T(8,128)S(1)}) all-reduce(f32[32,32]{0,1:T(8,128)S(1)} %convolution_bitcast_fusion.7, f32[32,32]{1,0:T(8,128)S(1)} %convolution_bitcast_fusion.8), channel_id=1, replica_groups=mesh['gx'=8,'gy'=4] {'gx','gy'}, use_global_device_ids=true, to_apply=%region_4.7 | all-reduce | flops 2048 | bytes 16384 | tf_op jit(solution)/shard_map/psum | solution.py:70
  108.9 0.6 convolution_subtract_fusion.4
  109.8 2.9 %cholesky.85 = f32[32,32]{1,0:T(8,128)S(1)} custom-call(f32[32,32]{1,0:T(8,128)S(1)} %fusion.36), custom_call_target="Cholesky" | custom-call | tf_op jit(solution)/shard_map/jit(cholesky)/cholesky | solution.py:43
  112.8 0.6 compare_reduce_fusion.2
  113.4 0.7 fusion.40
  114.1 2.4 custom-call.9
  117.4 2.6 %collective-permute-start.4 = (f32[32,1,16,128]{3,0,2,1:T(8,128)S(1)}, f32[32,1,16,128]{3,0,2,1:T(8,128)S(1)}, u32[]{:S(2)}, u32[]{:S(2)}) collective-permute-start(f32[32,1,16,128]{3,0,2,1:T(8,128)S(1)} %get-tuple-element.31), channel_id=1, source_target_pairs={{4,0},{8,4},{12,8},{16,12},{20,16},{24,20},{28,24},{0,28},{5,1},{9... | collective-permute-start | bytes 786440 | tf_op jit(solution)/shard_map/ppermute | solution.py:18
  120.3 3.9 %collective-permute-done.5 = f32[32,1,16,128]{3,0,2,1:T(8,128)S(1)} collective-permute-done((f32[32,1,16,128]{3,0,2,1:T(8,128)S(1)}, f32[32,1,16,128]{3,0,2,1:T(8,128)S(1)}, u32[]{:S(2)}, u32[]{:S(2)}) %collective-permute-start.5) | collective-permute-done | bytes 262176 | tf_op jit(solution)/shard_map/ppermute | solution.py:15
  124.2 1.6 collective-permute-done.4
  125.8 2.3 collective-permute-start.6
  128.6 2.0 collective-permute-done.6
  130.6 3.8 %collective-permute-done.7 = f32[32,4,1,128]{3,0,2,1:T(8,128)S(1)} collective-permute-done((f32[32,4,1,128]{3,0,2,1:T(8,128)S(1)}, f32[32,4,1,128]{3,0,2,1:T(8,128)S(1)}, u32[]{:S(2)}, u32[]{:S(2)}) %collective-permute-start.7) | collective-permute-done | bytes 65568 | tf_op jit(solution)/shard_map/ppermute | solution.py:15
  134.4 1.6 convolution_subtract_fusion.3
  137.1 38.9 %all-reduce.1 = (f32[32,32]{0,1:T(8,128)S(1)}, f32[32,32]{1,0:T(8,128)S(1)}) all-reduce(f32[32,32]{0,1:T(8,128)S(1)} %convolution_bitcast_fusion.4, f32[32,32]{1,0:T(8,128)S(1)} %convolution_bitcast_fusion.5), channel_id=1, replica_groups=mesh['gx'=8,'gy'=4] {'gx','gy'}, use_global_device_ids=true, to_apply=%region_6.9 | all-reduce | flops 2048 | bytes 16384 | tf_op jit(solution)/shard_map/psum | solution.py:70
  176.0 0.6 convolution_subtract_fusion.2
  177.0 2.9 %cholesky.96 = f32[32,32]{1,0:T(8,128)S(1)} custom-call(f32[32,32]{1,0:T(8,128)S(1)} %fusion.33), custom_call_target="Cholesky" | custom-call | tf_op jit(solution)/shard_map/jit(cholesky)/cholesky | solution.py:43
  179.9 0.6 compare_reduce_fusion.1
  180.5 0.7 fusion.41
  181.2 2.4 custom-call.10
  184.6 2.6 %collective-permute-start.8 = (f32[32,1,16,128]{3,0,2,1:T(8,128)S(1)}, f32[32,1,16,128]{3,0,2,1:T(8,128)S(1)}, u32[]{:S(2)}, u32[]{:S(2)}) collective-permute-start(f32[32,1,16,128]{3,0,2,1:T(8,128)S(1)} %get-tuple-element.25), channel_id=1, source_target_pairs={{4,0},{8,4},{12,8},{16,12},{20,16},{24,20},{28,24},{0,28},{5,1},{9... | collective-permute-start | bytes 786440 | tf_op jit(solution)/shard_map/ppermute | solution.py:18
  187.4 4.8 %collective-permute-done.9 = f32[32,1,16,128]{3,0,2,1:T(8,128)S(1)} collective-permute-done((f32[32,1,16,128]{3,0,2,1:T(8,128)S(1)}, f32[32,1,16,128]{3,0,2,1:T(8,128)S(1)}, u32[]{:S(2)}, u32[]{:S(2)}) %collective-permute-start.9) | collective-permute-done | bytes 262176 | tf_op jit(solution)/shard_map/ppermute | solution.py:15
  192.2 0.7 collective-permute-done.8
  193.0 2.3 collective-permute-start.10
  195.5 2.0 collective-permute-done.10
  197.5 4.0 %collective-permute-done.11 = f32[32,4,1,128]{3,0,2,1:T(8,128)S(1)} collective-permute-done((f32[32,4,1,128]{3,0,2,1:T(8,128)S(1)}, f32[32,4,1,128]{3,0,2,1:T(8,128)S(1)}, u32[]{:S(2)}, u32[]{:S(2)}) %collective-permute-start.11) | collective-permute-done | bytes 65568 | tf_op jit(solution)/shard_map/ppermute | solution.py:15
  201.5 1.6 convolution_subtract_fusion.1
  204.2 37.9 %all-reduce = (f32[32,32]{1,0:T(8,128)S(1)}, f32[32,32]{0,1:T(8,128)S(1)}) all-reduce(f32[32,32]{1,0:T(8,128)S(1)} %convolution_bitcast_fusion.2, f32[32,32]{0,1:T(8,128)S(1)} %convolution_bitcast_fusion.1), channel_id=1, replica_groups=mesh['gx'=8,'gy'=4] {'gx','gy'}, use_global_device_ids=true, to_apply=%region_7.10 | all-reduce | flops 2048 | bytes 16384 | tf_op jit(solution)/shard_map/psum | solution.py:70
  242.1 0.6 convolution_subtract_fusion
  243.0 2.9 %cholesky.107 = f32[32,32]{1,0:T(8,128)S(1)} custom-call(f32[32,32]{1,0:T(8,128)S(1)} %fusion.30), custom_call_target="Cholesky" | custom-call | tf_op jit(solution)/shard_map/jit(cholesky)/cholesky | solution.py:43
  246.0 0.6 compare_reduce_fusion
  246.6 0.7 select_bitcast_fusion
  247.3 2.4 custom-call.11
  250.5 1.1 copy.22
  251.6 0.7 copy.21
  252.4 0.6 pad_maximum_fusion.33
  (52 shorter events, 10.0 us)
Async XLA Ops:
  52.6 7.9 %collective-permute-start.1 = (f32[32,1,16,128]{3,0,2,1:T(8,128)S(1)}, f32[32,1,16,128]{3,0,2,1:T(8,128)S(1)}, u32[]{:S(2)}, u32[]{:S(2)}) collective-permute-start(f32[32,1,16,128]{3,0,2,1:T(8,128)S(1)} %get-tuple-element.36), channel_id=1, source_target_pairs={{0,4},{4,8},{8,12},{12,16},{16,20},{20,24},{24,28},{28,0},{1,5},{5... | collective-permute-start | bytes 786440 | tf_op jit(solution)/shard_map/ppermute | solution.py:15
  52.7 8.4 %collective-permute-start = (f32[32,1,16,128]{3,0,2,1:T(8,128)S(1)}, f32[32,1,16,128]{3,0,2,1:T(8,128)S(1)}, u32[]{:S(2)}, u32[]{:S(2)}) collective-permute-start(f32[32,1,16,128]{3,0,2,1:T(8,128)S(1)} %get-tuple-element.37), channel_id=1, source_target_pairs={{4,0},{8,4},{12,8},{16,12},{20,16},{24,20},{28,24},{0,28},{5,1},{9... | collective-permute-start | bytes 786440 | tf_op jit(solution)/shard_map/ppermute | solution.py:18
  55.7 7.6 %copy-start = (f32[2,16,128]{2,1,0:T(8,128)S(1)}, f32[2,16,128]{2,1,0:T(8,128)}, u32[]{:S(2)}) copy-start(f32[2,16,128]{2,1,0:T(8,128)} %param.6) | copy-start | bytes 49156
  61.1 4.3 %collective-permute-start.2 = (f32[32,4,1,128]{3,0,2,1:T(8,128)S(1)}, f32[32,4,1,128]{3,0,2,1:T(8,128)S(1)}, u32[]{:S(2)}, u32[]{:S(2)}) collective-permute-start(f32[32,4,1,128]{3,0,2,1:T(8,128)S(1)} %get-tuple-element.18), channel_id=1, source_target_pairs={{1,0},{2,1},{3,2},{0,3},{5,4},{6,5},{7,6},{4,7},{9,8},{10,9},{11,1... | collective-permute-start | bytes 196616 | tf_op jit(solution)/shard_map/ppermute | solution.py:18
  63.3 6.2 %collective-permute-start.3 = (f32[32,4,1,128]{3,0,2,1:T(8,128)S(1)}, f32[32,4,1,128]{3,0,2,1:T(8,128)S(1)}, u32[]{:S(2)}, u32[]{:S(2)}) collective-permute-start(f32[32,4,1,128]{3,0,2,1:T(8,128)S(1)} %get-tuple-element.19), channel_id=1, source_target_pairs={{0,1},{1,2},{2,3},{3,0},{4,5},{5,6},{6,7},{7,4},{8,9},{9,10},{10,1... | collective-permute-start | bytes 196616 | tf_op jit(solution)/shard_map/ppermute | solution.py:15
  117.4 6.8 %collective-permute-start.5 = (f32[32,1,16,128]{3,0,2,1:T(8,128)S(1)}, f32[32,1,16,128]{3,0,2,1:T(8,128)S(1)}, u32[]{:S(2)}, u32[]{:S(2)}) collective-permute-start(f32[32,1,16,128]{3,0,2,1:T(8,128)S(1)} %get-tuple-element.30), channel_id=1, source_target_pairs={{0,4},{4,8},{8,12},{12,16},{16,20},{20,24},{24,28},{28,0},{1,5},{5... | collective-permute-start | bytes 786440 | tf_op jit(solution)/shard_map/ppermute | solution.py:15
  117.4 8.4 %collective-permute-start.4 = (f32[32,1,16,128]{3,0,2,1:T(8,128)S(1)}, f32[32,1,16,128]{3,0,2,1:T(8,128)S(1)}, u32[]{:S(2)}, u32[]{:S(2)}) collective-permute-start(f32[32,1,16,128]{3,0,2,1:T(8,128)S(1)} %get-tuple-element.31), channel_id=1, source_target_pairs={{4,0},{8,4},{12,8},{16,12},{20,16},{24,20},{28,24},{0,28},{5,1},{9... | collective-permute-start | bytes 786440 | tf_op jit(solution)/shard_map/ppermute | solution.py:18
  125.8 4.8 %collective-permute-start.6 = (f32[32,4,1,128]{3,0,2,1:T(8,128)S(1)}, f32[32,4,1,128]{3,0,2,1:T(8,128)S(1)}, u32[]{:S(2)}, u32[]{:S(2)}) collective-permute-start(f32[32,4,1,128]{3,0,2,1:T(8,128)S(1)} %get-tuple-element.16), channel_id=1, source_target_pairs={{1,0},{2,1},{3,2},{0,3},{5,4},{6,5},{7,6},{4,7},{9,8},{10,9},{11,1... | collective-permute-start | bytes 196616 | tf_op jit(solution)/shard_map/ppermute | solution.py:18
  128.1 6.2 %collective-permute-start.7 = (f32[32,4,1,128]{3,0,2,1:T(8,128)S(1)}, f32[32,4,1,128]{3,0,2,1:T(8,128)S(1)}, u32[]{:S(2)}, u32[]{:S(2)}) collective-permute-start(f32[32,4,1,128]{3,0,2,1:T(8,128)S(1)} %get-tuple-element.17), channel_id=1, source_target_pairs={{0,1},{1,2},{2,3},{3,0},{4,5},{5,6},{6,7},{7,4},{8,9},{9,10},{10,1... | collective-permute-start | bytes 196616 | tf_op jit(solution)/shard_map/ppermute | solution.py:15
  184.5 7.7 %collective-permute-start.9 = (f32[32,1,16,128]{3,0,2,1:T(8,128)S(1)}, f32[32,1,16,128]{3,0,2,1:T(8,128)S(1)}, u32[]{:S(2)}, u32[]{:S(2)}) collective-permute-start(f32[32,1,16,128]{3,0,2,1:T(8,128)S(1)} %get-tuple-element.24), channel_id=1, source_target_pairs={{0,4},{4,8},{8,12},{12,16},{16,20},{20,24},{24,28},{28,0},{1,5},{5... | collective-permute-start | bytes 786440 | tf_op jit(solution)/shard_map/ppermute | solution.py:15
  184.6 8.4 %collective-permute-start.8 = (f32[32,1,16,128]{3,0,2,1:T(8,128)S(1)}, f32[32,1,16,128]{3,0,2,1:T(8,128)S(1)}, u32[]{:S(2)}, u32[]{:S(2)}) collective-permute-start(f32[32,1,16,128]{3,0,2,1:T(8,128)S(1)} %get-tuple-element.25), channel_id=1, source_target_pairs={{4,0},{8,4},{12,8},{16,12},{20,16},{24,20},{28,24},{0,28},{5,1},{9... | collective-permute-start | bytes 786440 | tf_op jit(solution)/shard_map/ppermute | solution.py:18
  193.0 4.5 %collective-permute-start.10 = (f32[32,4,1,128]{3,0,2,1:T(8,128)S(1)}, f32[32,4,1,128]{3,0,2,1:T(8,128)S(1)}, u32[]{:S(2)}, u32[]{:S(2)}) collective-permute-start(f32[32,4,1,128]{3,0,2,1:T(8,128)S(1)} %get-tuple-element.14), channel_id=1, source_target_pairs={{1,0},{2,1},{3,2},{0,3},{5,4},{6,5},{7,6},{4,7},{9,8},{10,9},{11,1... | collective-permute-start | bytes 196616 | tf_op jit(solution)/shard_map/ppermute | solution.py:18
  195.2 6.2 %collective-permute-start.11 = (f32[32,4,1,128]{3,0,2,1:T(8,128)S(1)}, f32[32,4,1,128]{3,0,2,1:T(8,128)S(1)}, u32[]{:S(2)}, u32[]{:S(2)}) collective-permute-start(f32[32,4,1,128]{3,0,2,1:T(8,128)S(1)} %get-tuple-element.15), channel_id=1, source_target_pairs={{0,1},{1,2},{2,3},{3,0},{4,5},{5,6},{6,7},{7,4},{8,9},{9,10},{10,1... | collective-permute-start | bytes 196616 | tf_op jit(solution)/shard_map/ppermute | solution.py:15
where the time goes:
time: 254 us; the launch traced here: 253 us
  blocking collectives  157 us (62%)
  waiting for transfers between devices  34.3 us (14%)
  other arithmetic  28.9 us (11%)
  starting transfers between devices  15.3 us (6%)
  matrix products  13.3 us (5%)
  local copies, waits for them, and re-layouts  3.44 us (1%)
    psum x3, blocking collectives, per_device(): lax.psum((inner_block(current, image), inner_block(image, image)), ('gx',...  115 us
    psum x1, blocking collectives, per_device(): probe_matrix = lax.psum(inner_block(probes, probes), ('gx', 'gy'))  42.1 us
    ppermute x6, waiting for transfers between devices, with_halo(): lax.ppermute(lax.slice_in_dim(block, block.shape[dim] - width, None, axis...  25.4 us
    ppermute x6, starting transfers between devices, with_halo(): lax.ppermute(lax.slice_in_dim(block, 0, width, axis=dim), axis, backward)  14.7 us
    another operation x12, other arithmetic, inverse_lower(): lower_factor = jnp.linalg.cholesky(gram_matrix)  14.4 us
    another operation x6, other arithmetic, inverse_lower(): lax.linalg.triangular_solve(lower_factor, identity_matrix, left_side=True...  11 us
    ppermute x6, waiting for transfers between devices, with_halo(): lax.ppermute(lax.slice_in_dim(block, 0, width, axis=dim), axis, backward)  8.93 us
    dot_general x9, matrix products, combine(): jnp.einsum('pxyz,pq->qxyz', vectors, matrix, precision=lax.Precision.HIGH...  7.62 us
  transfers between devices with their start and end apart: 12, of which 12 were waited for; matrix products, arithmetic and copies ran while one was open for 0% of the time, Pallas kernels for 0%

commit v1 on v0

v1 whole, which is shorter than its diff:
```python
import functools

import jax
import jax.numpy as jnp
from jax import lax
from jax.experimental import pallas as pl
from jax.experimental.pallas import tpu as pltpu
from jax.sharding import PartitionSpec as P

ITERS = 3
CHUNK = 8
CENTRE = 7.5
SCALE = 2.5
PANEL = 4
MESH = pl.DeviceIdType.MESH


def mm(left, right, left_dim=1, right_dim=0):
    return lax.dot_general(
        left,
        right,
        (((left_dim,), (right_dim,)), ((), ())),
        precision=lax.Precision.HIGHEST,
        preferred_element_type=jnp.float32,
    )


def factor(matrix):
    size = matrix.shape[0]
    rows = lax.broadcasted_iota(jnp.int32, (size, size), 0)
    columns = lax.broadcasted_iota(jnp.int32, (size, size), 1)
    upper = matrix
    inverse = jnp.where(rows == columns, 1.0, 0.0).astype(jnp.float32)
    for start in range(0, size, PANEL):
        panel = [
            jnp.broadcast_to(upper[:, start + m : start + m + 1], (size, size)) for m in range(PANEL)
        ]
        for m in range(PANEL):
            at = start + m
            pivot = panel[m][at : at + 1, :]
            root = lax.rsqrt(pivot)
            root = root * (1.5 - 0.5 * pivot * root * root)
            below = jnp.where(rows > at, panel[m] * root, 0.0)
            upper_row = upper[at : at + 1, :] * root
            inverse_row = inverse[at : at + 1, :] * root
            upper = jnp.where(rows == at, upper_row, upper - below * upper_row)
            inverse = jnp.where(rows == at, inverse_row, inverse - below * inverse_row)
            for later in range(m + 1, PANEL):
                panel[later] = panel[later] - below * below[start + later : start + later + 1, :]
    return jnp.where(columns >= rows, upper, 0.0), inverse


def kernel(
    nx, ny, probes_ref, diagonal_ref, alphas_ref, betas_ref, next_ref,
    fields, split, moments, part_x, part_y, total,
    send_halo, recv_halo, send_sum, recv_sum, send_z, recv_z, send_all, recv_all,
):
    chunks, planes, lines = probes_ref.shape[0], probes_ref.shape[1], probes_ref.shape[2]
    probes = chunks * CHUNK
    gx, gy = lax.axis_index("gx"), lax.axis_index("gy")

    def x_device(offset):
        return lax.rem(gx + offset, nx)

    def y_device(offset):
        return lax.rem(gy + offset, ny)

    barrier = pltpu.get_barrier_semaphore()
    for offset in range(1, nx):
        pl.semaphore_signal(barrier, inc=1, device_id={"gx": x_device(offset)}, device_id_type=MESH)
    for offset in range(1, ny):
        pl.semaphore_signal(barrier, inc=1, device_id={"gy": y_device(offset)}, device_id_type=MESH)
    pl.semaphore_wait(barrier, nx + ny - 2)

    inner_x, inner_y = pl.ds(1, planes), pl.ds(1, lines)

    def halo_copies(step):
        here = fields.at[step]
        moves = (
            (here.at[planes, inner_y], here.at[0, inner_y], {"gx": x_device(1)}),
            (here.at[1, inner_y], here.at[planes + 1, inner_y], {"gx": x_device(nx - 1)}),
            (here.at[inner_x, lines], here.at[inner_x, 0], {"gy": y_device(1)}),
            (here.at[inner_x, 1], here.at[inner_x, lines + 1], {"gy": y_device(ny - 1)}),
        )
        return [
            pltpu.make_async_remote_copy(
                src_ref=source,
                dst_ref=target,
                send_sem=send_halo.at[step, side],
                recv_sem=recv_halo.at[step, side],
                device_id=device,
                device_id_type=MESH,
            )
            for side, (source, target, device) in enumerate(moves)
        ]

    def load_chunk(chunk, carry):
        for x in range(planes):
            for y in range(lines):
                fields[chunk, x + 1, y + 1] = probes_ref[chunk, x, y]
        for copy in halo_copies(chunk):
            copy.start()
        return carry

    lax.fori_loop(0, chunks, load_chunk, 0)

    def split_level(level):
        for x in range(planes):
            for y in range(lines):
                value = jnp.concatenate(
                    [fields[level * chunks + c, x + 1, y + 1] for c in range(chunks)], axis=0
                )
                high = value.astype(jnp.bfloat16)
                low = (value - high.astype(jnp.float32)).astype(jnp.bfloat16)
                lanes = pl.ds((x * lines + y) * value.shape[1], value.shape[1])
                split[level, 0:probes, lanes] = high
                split[level, probes : 2 * probes, lanes] = low

    def gram(left, right):
        product = lax.dot_general(
            split[left], split[right], (((1,), (1,)), ((), ())), preferred_element_type=jnp.float32
        )
        return (
            (product[probes:, probes:] + (product[:probes, probes:] + product[probes:, :probes]))
            + product[:probes, :probes]
        )

    grams = []
    for level in range(ITERS):

        def apply_chunk(chunk, carry, level=level):
            step = level * chunks + chunk
            for copy in halo_copies(step):
                copy.wait_recv()
            for x in range(1, planes + 1):
                for y in range(1, lines + 1):
                    value = fields[step, x, y]
                    beside = fields[step, x - 1, y] + fields[step, x + 1, y]
                    beside = beside + (fields[step, x, y - 1] + fields[step, x, y + 1])
                    beside = beside + (
                        pltpu.roll(value, 1, 1) + pltpu.roll(value, value.shape[1] - 1, 1)
                    )
                    own = jnp.broadcast_to(diagonal_ref[x - 1, y - 1 : y, :], value.shape)
                    fields[step + chunks, x, y] = own * value - beside * (1.0 / SCALE)
            if level + 1 < ITERS:
                for copy in halo_copies(step + chunks):
                    copy.start()
            return carry

        if level == 0:
            split_level(0)
            grams.append(gram(0, 0))
        lax.fori_loop(0, chunks, apply_chunk, 0)
        split_level(level + 1)
        grams.append(gram(level, level + 1))
        grams.append(gram(level + 1, level + 1))

    zero = jnp.zeros_like(grams[0])
    width = moments.shape[1]
    per_row = width // probes
    grams_padded = grams + [zero] * (-len(grams) % per_row)
    bands = len(grams_padded) // per_row
    for band in range(bands):
        moments[band * probes : (band + 1) * probes, :] = jnp.concatenate(
            grams_padded[band * per_row : (band + 1) * per_row], axis=1
        )
    piece = moments.shape[0] // nx
    if moments.shape[0] > bands * probes:
        moments[bands * probes :, :] = jnp.zeros_like(moments[bands * probes :, :])

    def rows_of(index):
        return pl.ds(pl.multiple_of(index * piece, piece), piece)

    copies = []
    for offset in range(1, nx):
        copies.append(
            pltpu.make_async_remote_copy(
                src_ref=moments.at[rows_of(x_device(offset))],
                dst_ref=part_x.at[offset],
                send_sem=send_sum.at[offset],
                recv_sem=recv_sum.at[offset],
                device_id={"gx": x_device(offset)},
                device_id_type=MESH,
            )
        )
        copies[-1].start()
    partial = moments[rows_of(gx), :]
    for offset in range(1, nx):
        copies[offset - 1].wait_recv()
        partial = partial + part_x[offset]
    part_y[gy] = partial
    copies_y = []
    for offset in range(1, ny):
        copies_y.append(
            pltpu.make_async_remote_copy(
                src_ref=part_y.at[gy],
                dst_ref=part_y.at[gy],
                send_sem=send_z.at[offset],
                recv_sem=recv_z.at[offset],
                device_id={"gy": y_device(offset)},
                device_id_type=MESH,
            )
        )
        copies_y[-1].start()
    for copy in copies_y:
        copy.wait_recv()
    whole = part_y[0]
    for index in range(1, ny):
        whole = whole + part_y[index]
    total[rows_of(gx), :] = whole
    copies_all = []
    for offset in range(1, nx):
        copies_all.append(
            pltpu.make_async_remote_copy(
                src_ref=total.at[rows_of(gx)],
                dst_ref=total.at[rows_of(gx)],
                send_sem=send_all.at[offset],
                recv_sem=recv_all.at[offset],
                device_id={"gx": x_device(offset)},
                device_id_type=MESH,
            )
        )
        copies_all[-1].start()
    for copy in copies_all:
        copy.wait_recv()

    moment = []
    for index in range(len(grams)):
        band, place = index // per_row, index % per_row
        block = total[band * probes : (band + 1) * probes, :]
        moment.append(block[:, place * probes : (place + 1) * probes])

    levels = ITERS + 1
    lower = {}
    uppers, inverses = [], []
    for j in range(levels):
        pivot = moment[2 * j]
        for i in range(j):
            pivot = pivot - mm(lower[j, i], lower[j, i], 1, 1)
        upper, inverse = factor(pivot)
        uppers.append(upper)
        inverses.append(inverse)
        for k in range(j + 1, levels):
            rest = moment[j + k]
            for i in range(j):
                rest = rest - mm(lower[k, i], lower[j, i], 1, 1)
            lower[k, j] = mm(rest, inverse, 1, 1)

    rows = lax.broadcasted_iota(jnp.int32, (probes, probes), 0)
    columns = lax.broadcasted_iota(jnp.int32, (probes, probes), 1)
    shift = jnp.where(rows == columns, CENTRE, 0.0).astype(jnp.float32)
    before = None
    for j in range(ITERS):
        inside = lower[j + 1, j]
        if before is not None:
            inside = inside - mm(lower[j, j - 1], before, 1, 1)
        alphas_ref[j] = shift + SCALE * mm(inverses[j], inside)
        before = mm(uppers[j + 1], inverses[j], 1, 1)
        betas_ref[j] = SCALE * before

    mixing = [None] * levels
    mixing[ITERS] = inverses[ITERS]
    for k in range(ITERS - 1, -1, -1):
        gathered = mm(mixing[ITERS], lower[ITERS, k])
        for i in range(k + 1, ITERS):
            gathered = gathered + mm(mixing[i], lower[i, k])
        mixing[k] = -mm(gathered, inverses[k])
    pieces = []
    for block in mixing:
        high = block.astype(jnp.bfloat16)
        pieces.append((high, (block - high.astype(jnp.float32)).astype(jnp.bfloat16)))
    weights = jnp.concatenate(
        [jnp.concatenate([part[side] for part in pieces for _ in range(2)], axis=1) for side in range(2)],
        axis=0,
    )
    lanes = next_ref.shape[2]
    group = 4
    basis = split.at[...].reshape(levels * 2 * probes, split.shape[2])
    for start in range(0, planes * lines, group):
        product = jnp.dot(
            weights,
            basis[:, start * lanes : (start + group) * lanes],
            preferred_element_type=jnp.float32,
        )
        product = product[:probes] + product[probes:]
        for inner in range(group):
            next_ref[start + inner] = product[:, inner * lanes : (inner + 1) * lanes]

    def finish(step, carry):
        for copy in halo_copies(step):
            copy.wait_send()
        return carry

    lax.fori_loop(0, ITERS * chunks, finish, 0)
    for copy in copies + copies_y + copies_all:
        copy.wait_send()


def per_device(nx, ny, probe_signs, diagonal):
    probes, planes, lines, lanes = probe_signs.shape
    chunks = probes // CHUNK
    signs = 2.0 * probe_signs.astype(jnp.float32) - 1.0
    signs = signs.reshape(chunks, CHUNK, planes, lines, lanes).transpose(0, 2, 3, 1, 4)
    own = (6.0 - CENTRE + diagonal) * (1.0 / SCALE)
    levels = ITERS + 1
    bands = -(-(2 * ITERS + 1) * probes // lanes)
    rows = max(bands * probes, 8 * nx)
    piece = rows // nx
    small = jax.ShapeDtypeStruct((ITERS, probes, probes), jnp.float32)
    vmem = pl.BlockSpec(memory_space=pltpu.VMEM)
    dma = pltpu.SemaphoreType.DMA
    alphas, betas, block = pl.pallas_call(
        functools.partial(kernel, nx, ny),
        out_shape=(
            small,
            small,
            jax.ShapeDtypeStruct((planes * lines, probes, lanes), jnp.float32),
        ),
        in_specs=[vmem, vmem],
        out_specs=(vmem, vmem, vmem),
        scratch_shapes=[
            pltpu.VMEM((levels * chunks, planes + 2, lines + 2, CHUNK, lanes), jnp.float32),
            pltpu.VMEM((levels, 2 * probes, planes * lines * lanes), jnp.bfloat16),
            pltpu.VMEM((rows, lanes), jnp.float32),
            pltpu.VMEM((nx, piece, lanes), jnp.float32),
            pltpu.VMEM((ny, piece, lanes), jnp.float32),
            pltpu.VMEM((rows, lanes), jnp.float32),
            dma((ITERS * chunks, 4)),
            dma((ITERS * chunks, 4)),
            dma((nx,)),
            dma((nx,)),
            dma((ny,)),
            dma((ny,)),
            dma((nx,)),
            dma((nx,)),
        ],
        compiler_params=pltpu.CompilerParams(collective_id=0, has_side_effects=True),
        name="lanczos",
    )(signs, own)
    block = block.reshape(planes, lines, probes, lanes).transpose(2, 0, 1, 3)
    return alphas, betas, block


def solution(mesh):
    nx, ny = mesh.shape["gx"], mesh.shape["gy"]
    in_specs = (P(None, "gx", "gy", None), P("gx", "gy", None))
    out_specs = (P(), P(), P(None, "gx", "gy", None))
    return jax.shard_map(
        functools.partial(per_device, nx, ny),
        mesh=mesh,
        in_specs=in_specs,
        out_specs=out_specs,
        check_vma=False,
    )
```

time: 254 us -> 53.2 us (0.21)
  blocking collectives: 157 us -> 0 us
  Pallas kernels: 0 us -> 45.1 us
  waiting for transfers between devices: 34.3 us -> 0 us
  other arithmetic: 28.9 us -> 2.43 us
  starting transfers between devices: 15.3 us -> 0 us
  matrix products: 13.3 us -> 0 us
    psum x4 -> x0, blocking collectives: 157 us -> none  [the longest x3 115 us: per_device(): lax.psum((inner_block(current, image), inner_block(image, image)), ('gx',...]
    pallas_call x0 -> x1, Pallas kernels: none -> 45.1 us  [per_device(): pl.pallas_call(functools.partial(kernel, nx, ny), out_shape=(small, small...]
    ppermute x12 -> x0, waiting for transfers between devices: 34.3 us -> none  [the longest x6 25.4 us: with_halo(): lax.ppermute(lax.slice_in_dim(block, block.shape[dim] - width, None, axis...]
    another operation x22 -> x0, other arithmetic: 27.4 us -> none  [the longest x12 14.4 us: inverse_lower(): lower_factor = jnp.linalg.cholesky(gram_matrix)]
    ppermute x12 -> x0, starting transfers between devices: 15.3 us -> none  [the longest x6 14.7 us: with_halo(): lax.ppermute(lax.slice_in_dim(block, 0, width, axis=dim), axis, backward)]
    dot_general x19 -> x0, matrix products: 12.4 us -> none  [the longest x9 7.62 us: combine(): jnp.einsum('pxyz,pq->qxyz', vectors, matrix, precision=lax.Precision.HIGH...]
    reshape x0 -> x2, local copies, waits for them, and re-layouts: none -> 3.26 us  [the longest x1 2.15 us: per_device(): block = block.reshape(planes, lines, probes, lanes).transpose(2, 0, 1, 3)]
  transfers between devices with their start and end apart: 12 -> 0, of which waited for: 12 -> 0; matrix products, arithmetic and copies ran while one was open for 0% -> 0% of each run, Pallas kernels for 0% -> 0%
where the time goes in v1:
time: 53.2 us; the launch traced here: 52.9 us
  Pallas kernels  45.1 us (85%)
  local copies, waits for them, and re-layouts  4.7 us (9%)
  other arithmetic  2.43 us (5%)
  between operations  0.66 us (1%)
    pallas_call x1, Pallas kernels, per_device(): pl.pallas_call(functools.partial(kernel, nx, ny), out_shape=(small, small...  45.1 us
    reshape x1, local copies, waits for them, and re-layouts, per_device(): block = block.reshape(planes, lines, probes, lanes).transpose(2, 0, 1, 3)  2.15 us
    unnamed x6, local copies, waits for them, and re-layouts  1.44 us
    mul x1, other arithmetic, per_device(): own = (6.0 - CENTRE + diagonal) * (1.0 / SCALE)  1.33 us
    sub x1, other arithmetic, per_device(): signs = 2.0 * probe_signs.astype(jnp.float32) - 1.0  1.1 us
    reshape x1, local copies, waits for them, and re-layouts, per_device(): signs.reshape(chunks, CHUNK, planes, lines, lanes).transpose(0, 2, 3, 1, 4)  1.1 us

profile of v1, /device:TPU:0, one launch (start us, length us, event | category | flops | bytes accessed | tf_op | source)
XLA Modules:
  0.0 52.9 jit_solution(972222049617950673)
XLA Ops:
  0.6 1.3 %add_multiply_fusion.diagonal_ref = f32[2,16,128]{2,1,0:T(8,128)} fusion(f32[2,16,128]{2,1,0:T(8,128)} %param.3), kind=kLoop, calls=%fused_computation.3 | loop fusion | flops 8192 | bytes 32768 | tf_op jit(solution)/shard_map/mul | solution.py:304
  2.0 1.1 %multiply_add_fusion = f32[32,2,16,128]{3,2,1,0:T(8,128)S(1)} fusion(s32[32,2,16,128]{3,2,1,0:T(8,128)} %param.2), kind=kLoop, calls=%fused_computation.2 | loop fusion | flops 393216 | bytes 1048576 | tf_op jit(solution)/shard_map/sub | solution.py:302
  3.1 1.1 %copy.11 = f32[4,8,2,16,128]{4,1,3,2,0:T(8,128)} copy(f32[4,8,2,16,128]{4,3,2,1,0:T(8,128)S(1)} %bitcast.9) | data formatting | bytes 1048576 | tf_op jit(solution)/shard_map/reshape | solution.py:303
  4.2 45.1 %lanczos.1 = (f32[3,32,32]{2,1,0:T(8,128)}, f32[3,32,32]{2,1,0:T(8,128)}, f32[32,32,128]{2,1,0:T(8,128)}) custom-call(f32[4,2,16,8,128]{4,3,2,1,0:T(8,128)} %bitcast.8, f32[2,16,128]{2,1,0:T(8,128)} %add_multiply_fusion.diagonal_ref), custom_call_target="tpu_custom_call" | custom-call | tf_op jit(solution)/shard_map/lanczos/pallas_call | solution.py:312
  49.3 0.0 copy-start.1
  49.3 2.2 %copy.10 = f32[2,16,32,128]{3,1,0,2:T(8,128)} copy(f32[2,16,32,128]{3,2,1,0:T(8,128)} %bitcast.11) | data formatting | bytes 1048576 | tf_op jit(solution)/shard_map/reshape | solution.py:340
  51.5 0.0 copy-done.1
  51.5 0.0 copy-start
  51.5 0.6 %copy.14 = f32[3,32,32]{2,1,0:T(8,128)} copy(f32[3,32,32]{2,1,0:T(8,128)S(1)} %copy-done.1) | data formatting | bytes 24576
  52.1 0.2 copy-done
  52.3 0.6 %copy.15 = f32[3,32,32]{2,1,0:T(8,128)} copy(f32[3,32,32]{2,1,0:T(8,128)S(1)} %copy-done) | data formatting | bytes 24576
Async XLA Ops:
  49.3 2.2 %copy-start.1 = (f32[3,32,32]{2,1,0:T(8,128)S(1)}, f32[3,32,32]{2,1,0:T(8,128)}, u32[]{:S(2)}) copy-start(f32[3,32,32]{2,1,0:T(8,128)} %get-tuple-element.12) | copy-start | bytes 36868
  51.5 0.8 %copy-start = (f32[3,32,32]{2,1,0:T(8,128)S(1)}, f32[3,32,32]{2,1,0:T(8,128)}, u32[]{:S(2)}) copy-start(f32[3,32,32]{2,1,0:T(8,128)} %get-tuple-element.13) | copy-start | bytes 36868

commit v2 on v1

v2 whole, which is shorter than its diff:
```python
import functools

import jax
import jax.numpy as jnp
from jax import lax
from jax.experimental import pallas as pl
from jax.experimental.pallas import tpu as pltpu
from jax.sharding import PartitionSpec as P

ITERS = 3
CHUNK = 8
CENTRE = 7.5
SCALE = 2.5
PANEL = 4
VMEM_BYTES = 24 * 1024 * 1024
MESH = pl.DeviceIdType.MESH


def mm(left, right, left_dim=1, right_dim=0):
    return lax.dot_general(
        left,
        right,
        (((left_dim,), (right_dim,)), ((), ())),
        precision=lax.Precision.HIGHEST,
        preferred_element_type=jnp.float32,
    )


def factor(matrix):
    size = matrix.shape[0]
    rows = lax.broadcasted_iota(jnp.int32, (size, size), 0)
    columns = lax.broadcasted_iota(jnp.int32, (size, size), 1)
    upper = matrix
    inverse = jnp.where(rows == columns, 1.0, 0.0).astype(jnp.float32)
    for start in range(0, size, PANEL):
        panel = [
            jnp.broadcast_to(upper[:, start + m : start + m + 1], (size, size)) for m in range(PANEL)
        ]
        for m in range(PANEL):
            at = start + m
            pivot = panel[m][at : at + 1, :]
            root = lax.rsqrt(pivot)
            root = root * (1.5 - 0.5 * pivot * root * root)
            below = jnp.where(rows > at, panel[m] * root, 0.0)
            upper_row = upper[at : at + 1, :] * root
            inverse_row = inverse[at : at + 1, :] * root
            upper = jnp.where(rows == at, upper_row, upper - below * upper_row)
            inverse = jnp.where(rows == at, inverse_row, inverse - below * inverse_row)
            for later in range(m + 1, PANEL):
                panel[later] = panel[later] - below * below[start + later : start + later + 1, :]
    return jnp.where(columns >= rows, upper, 0.0), inverse


def pack(matrix, lanes):
    per = lanes // matrix.shape[1]
    rows = matrix.shape[0] // per
    return jnp.concatenate([matrix[i * rows : (i + 1) * rows] for i in range(per)], axis=1)


def unpack(packed, size):
    per = packed.shape[1] // size
    return jnp.concatenate([packed[:, i * size : (i + 1) * size] for i in range(per)], axis=0)


def kernel(
    nx, ny, signs_ref, diagonal_ref, alphas_ref, betas_ref, next_ref,
    fields, split, part_x, part_y,
    send_halo, recv_halo, send_x, recv_x, send_y, recv_y,
):
    planes, lines, lanes = diagonal_ref.shape
    cells = planes * lines
    probes = signs_ref.shape[0] // cells
    chunks = probes // CHUNK
    gx, gy = lax.axis_index("gx"), lax.axis_index("gy")

    def x_device(offset):
        return lax.rem(gx + offset, nx)

    def y_device(offset):
        return lax.rem(gy + offset, ny)

    barrier = pltpu.get_barrier_semaphore()
    for offset in range(1, nx):
        pl.semaphore_signal(barrier, inc=1, device_id={"gx": x_device(offset)}, device_id_type=MESH)
    for offset in range(1, ny):
        pl.semaphore_signal(barrier, inc=1, device_id={"gy": y_device(offset)}, device_id_type=MESH)

    inner_x, inner_y = pl.ds(1, planes), pl.ds(1, lines)

    def halo_copies(step):
        here = fields.at[step]
        moves = (
            (here.at[planes, inner_y], here.at[0, inner_y], {"gx": x_device(1)}),
            (here.at[1, inner_y], here.at[planes + 1, inner_y], {"gx": x_device(nx - 1)}),
            (here.at[inner_x, lines], here.at[inner_x, 0], {"gy": y_device(1)}),
            (here.at[inner_x, 1], here.at[inner_x, lines + 1], {"gy": y_device(ny - 1)}),
        )
        return [
            pltpu.make_async_remote_copy(
                src_ref=source,
                dst_ref=target,
                send_sem=send_halo.at[step, side],
                recv_sem=recv_halo.at[step, side],
                device_id=device,
                device_id_type=MESH,
            )
            for side, (source, target, device) in enumerate(moves)
        ]

    def load_chunk(chunk):
        for x in range(planes):
            for y in range(lines):
                start = chunk * CHUNK * cells + x * lines + y
                bits = signs_ref[pl.ds(start, CHUNK, stride=cells), :]
                fields[chunk, x + 1, y + 1] = 2.0 * bits.astype(jnp.float32) - 1.0

    load_chunk(0)
    pl.semaphore_wait(barrier, nx + ny - 2)
    for chunk in range(chunks):
        if chunk > 0:
            load_chunk(chunk)
        for copy in halo_copies(chunk):
            copy.start()

    def split_level(level):
        for x in range(planes):
            for y in range(lines):
                value = jnp.concatenate(
                    [fields[level * chunks + c, x + 1, y + 1] for c in range(chunks)], axis=0
                )
                high = value.astype(jnp.bfloat16)
                low = (value - high.astype(jnp.float32)).astype(jnp.bfloat16)
                at = pl.ds((x * lines + y) * lanes, lanes)
                split[level, 0:probes, at] = high
                split[level, probes : 2 * probes, at] = low

    def gram(left, right):
        product = lax.dot_general(
            split[left], split[right], (((1,), (1,)), ((), ())), preferred_element_type=jnp.float32
        )
        return (
            (product[probes:, probes:] + (product[:probes, probes:] + product[probes:, :probes]))
            + product[:probes, :probes]
        )

    height = part_x.shape[2] // 2

    def along(group, count, offset, part, send, recv, me, device):
        rows = pl.ds(0, height * count)
        return pltpu.make_async_remote_copy(
            src_ref=part.at[group, me, rows],
            dst_ref=part.at[group, me, rows],
            send_sem=send.at[group, offset],
            recv_sem=recv.at[group, offset],
            device_id=device,
            device_id_type=MESH,
        )

    def x_copies(group, count):
        return [
            along(group, count, o, part_x, send_x, recv_x, gx, {"gx": x_device(o)})
            for o in range(1, nx)
        ]

    def y_copies(group, count):
        return [
            along(group, count, o, part_y, send_y, recv_y, gy, {"gy": y_device(o)})
            for o in range(1, ny)
        ]

    def begin(group, matrices):
        for i, matrix in enumerate(matrices):
            part_x[group, gx, i * height : (i + 1) * height] = pack(matrix, lanes)
        for copy in x_copies(group, len(matrices)):
            copy.start()

    def added(part, group, count, slots):
        value = part[group, 0, 0 : height * count]
        for slot in range(1, slots):
            value = value + part[group, slot, 0 : height * count]
        return value

    def middle(group, count):
        for copy in x_copies(group, count):
            copy.wait_recv()
        part_y[group, gy, 0 : height * count] = added(part_x, group, count, nx)
        for copy in y_copies(group, count):
            copy.start()

    def end(group, count):
        for copy in y_copies(group, count):
            copy.wait_recv()
        value = added(part_y, group, count, ny)
        return [unpack(value[i * height : (i + 1) * height], probes) for i in range(count)]

    def apply_level(level):
        def apply_chunk(chunk, carry):
            step = level * chunks + chunk
            for copy in halo_copies(step):
                copy.wait_recv()
            for x in range(1, planes + 1):
                for y in range(1, lines + 1):
                    value = fields[step, x, y]
                    beside = fields[step, x - 1, y] + fields[step, x + 1, y]
                    beside = beside + (fields[step, x, y - 1] + fields[step, x, y + 1])
                    beside = beside + (pltpu.roll(value, 1, 1) + pltpu.roll(value, lanes - 1, 1))
                    own = (diagonal_ref[x - 1, y - 1 : y, :] + (6.0 - CENTRE)) * (1.0 / SCALE)
                    fields[step + chunks, x, y] = (
                        jnp.broadcast_to(own, value.shape) * value - beside * (1.0 / SCALE)
                    )
            if level + 1 < ITERS:
                for copy in halo_copies(step + chunks):
                    copy.start()
            return carry

        lax.fori_loop(0, chunks, apply_chunk, 0)

    levels = ITERS + 1
    moment = []
    lower, inverse_of = {}, {}
    uppers, inverses, before = [], [], []
    rows = lax.broadcasted_iota(jnp.int32, (probes, probes), 0)
    columns = lax.broadcasted_iota(jnp.int32, (probes, probes), 1)
    shift = jnp.where(rows == columns, CENTRE, 0.0).astype(jnp.float32)

    def schur(k, j, matrix):
        for i in range(j):
            matrix = matrix - mm(lower[k, i], lower[j, i], 1, 1)
        return matrix

    def factor_level(j):
        upper, inverse = factor(schur(j, j, moment[2 * j]))
        uppers.append(upper)
        inverses.append(inverse)

    def link(k, j):
        lower[k, j] = mm(schur(k, j, moment[j + k]), inverses[j], 1, 1)

    def coefficients(j):
        inside = lower[j + 1, j]
        if j > 0:
            inside = inside - mm(lower[j, j - 1], before[j - 1], 1, 1)
        alphas_ref[j] = shift + SCALE * mm(inverses[j], inside)

    def coupling(j):
        before.append(mm(uppers[j + 1], inverses[j], 1, 1))
        betas_ref[j] = SCALE * before[j]

    def invert_row(j):
        inverse_of[j, j] = inverses[j]
        for k in range(j):
            gathered = mm(lower[j, k], inverse_of[k, k])
            for i in range(k + 1, j):
                gathered = gathered + mm(lower[j, i], inverse_of[i, k])
            inverse_of[j, k] = -mm(inverses[j], gathered)

    split_level(0)
    begin(0, [gram(0, 0)])
    apply_level(0)
    split_level(1)
    begin(1, [gram(0, 1), gram(1, 1)])
    middle(0, 1)
    apply_level(1)
    split_level(2)
    begin(2, [gram(1, 2), gram(2, 2)])
    middle(1, 2)
    moment.extend(end(0, 1))
    factor_level(0)
    apply_level(2)
    middle(2, 2)
    split_level(3)
    begin(3, [gram(2, 3), gram(3, 3)])
    moment.extend(end(1, 2))
    link(1, 0)
    link(2, 0)
    factor_level(1)
    coefficients(0)
    coupling(0)
    middle(3, 2)
    moment.extend(end(2, 2))
    link(3, 0)
    link(2, 1)
    link(3, 1)
    factor_level(2)
    coefficients(1)
    coupling(1)
    for j in range(3):
        invert_row(j)
    known = [
        mm(lower[3, 0], inverse_of[0, 0]) + mm(lower[3, 1], inverse_of[1, 0]),
        mm(lower[3, 1], inverse_of[1, 1]),
        None,
    ]
    moment.extend(end(3, 2))
    link(3, 2)
    factor_level(3)
    mixing = []
    for k in range(3):
        gathered = mm(lower[3, 2], inverse_of[2, k])
        if known[k] is not None:
            gathered = gathered + known[k]
        mixing.append(-mm(inverses[3], gathered))
    mixing.append(inverses[3])
    coefficients(2)
    coupling(2)

    pieces = []
    for block in mixing:
        high = block.astype(jnp.bfloat16)
        pieces.append((high, (block - high.astype(jnp.float32)).astype(jnp.bfloat16)))
    weights = jnp.concatenate(
        [jnp.concatenate([part[side] for part in pieces for _ in range(2)], axis=1) for side in range(2)],
        axis=0,
    )
    group = 4
    basis = split.at[...].reshape(levels * 2 * probes, split.shape[2])
    for start in range(0, cells, group):
        product = jnp.dot(
            weights,
            basis[:, start * lanes : (start + group) * lanes],
            preferred_element_type=jnp.float32,
        )
        product = product[:probes] + product[probes:]
        for inner in range(group):
            next_ref[pl.ds(start + inner, probes, stride=cells), :] = product[
                :, inner * lanes : (inner + 1) * lanes
            ]

    def finish(step, carry):
        for copy in halo_copies(step):
            copy.wait_send()
        return carry

    lax.fori_loop(0, ITERS * chunks, finish, 0)
    for index, count in enumerate((1, 2, 2, 2)):
        for copy in x_copies(index, count) + y_copies(index, count):
            copy.wait_send()


def per_device(nx, ny, probe_signs, diagonal):
    probes, planes, lines, lanes = probe_signs.shape
    chunks = probes // CHUNK
    levels = ITERS + 1
    height = probes * probes // lanes
    cells = planes * lines
    small = jax.ShapeDtypeStruct((ITERS, probes, probes), jnp.float32)
    vmem = pl.BlockSpec(memory_space=pltpu.VMEM)
    dma = pltpu.SemaphoreType.DMA
    alphas, betas, block = pl.pallas_call(
        functools.partial(kernel, nx, ny),
        out_shape=(small, small, jax.ShapeDtypeStruct((probes * cells, lanes), jnp.float32)),
        in_specs=[vmem, vmem],
        out_specs=(vmem, vmem, vmem),
        scratch_shapes=[
            pltpu.VMEM((levels * chunks, planes + 2, lines + 2, CHUNK, lanes), jnp.float32),
            pltpu.VMEM((levels, 2 * probes, cells * lanes), jnp.bfloat16),
            pltpu.VMEM((levels, nx, 2 * height, lanes), jnp.float32),
            pltpu.VMEM((levels, ny, 2 * height, lanes), jnp.float32),
            dma((ITERS * chunks, 4)),
            dma((ITERS * chunks, 4)),
            dma((levels, nx)),
            dma((levels, nx)),
            dma((levels, ny)),
            dma((levels, ny)),
        ],
        compiler_params=pltpu.CompilerParams(
            collective_id=0, has_side_effects=True, vmem_limit_bytes=VMEM_BYTES
        ),
        name="lanczos",
    )(probe_signs.reshape(probes * cells, lanes), diagonal)
    return alphas, betas, block.reshape(probes, planes, lines, lanes)


def solution(mesh):
    nx, ny = mesh.shape["gx"], mesh.shape["gy"]
    in_specs = (P(None, "gx", "gy", None), P("gx", "gy", None))
    out_specs = (P(), P(), P(None, "gx", "gy", None))
    return jax.shard_map(
        functools.partial(per_device, nx, ny),
        mesh=mesh,
        in_specs=in_specs,
        out_specs=out_specs,
        check_vma=False,
    )
```

time: 53.2 us -> 43.1 us (0.81)
  Pallas kernels: 45.1 us -> 38.4 us
  other arithmetic: 2.43 us -> 0 us
  local copies, waits for them, and re-layouts: 4.7 us -> 3.79 us
    pallas_call x1, Pallas kernels: 45.1 us -> 38.4 us  [per_device(): pl.pallas_call(functools.partial(kernel, nx, ny), out_shape=(small, small...]
    reshape x2 -> x0, local copies, waits for them, and re-layouts: 3.26 us -> none  [the longest x1 2.15 us: per_device(): block = block.reshape(planes, lines, probes, lanes).transpose(2, 0, 1, 3)]
    unnamed x6 -> x7, local copies, waits for them, and re-layouts: 1.44 us -> 3.79 us
    mul x1 -> x0, other arithmetic: 1.33 us -> none  [per_device(): own = (6.0 - CENTRE + diagonal) * (1.0 / SCALE)]
    sub x1 -> x0, other arithmetic: 1.1 us -> none  [per_device(): signs = 2.0 * probe_signs.astype(jnp.float32) - 1.0]
where the time goes in v2:
time: 43.1 us; the launch traced here: 42.9 us
  Pallas kernels  38.4 us (89%)
  local copies, waits for them, and re-layouts  3.79 us (9%)
  between operations  0.65 us (2%)
    pallas_call x1, Pallas kernels, per_device(): pl.pallas_call(functools.partial(kernel, nx, ny), out_shape=(small, small...  38.4 us
    unnamed x7, local copies, waits for them, and re-layouts  3.79 us

profile of v2, /device:TPU:0, one launch (start us, length us, event | category | flops | bytes accessed | tf_op | source)
XLA Modules:
  0.0 42.9 jit_solution(12261280723298423495)
XLA Ops:
  0.6 0.0 copy-start
  0.6 1.0 %copy-done = s32[32,2,16,128]{3,2,1,0:T(8,128)S(1)} copy-done((s32[32,2,16,128]{3,2,1,0:T(8,128)S(1)}, s32[32,2,16,128]{3,2,1,0:T(8,128)}, u32[]{:S(2)}) %copy-start) | copy-done | bytes 524312
  1.7 0.0 copy-start.1
  1.7 0.7 %copy-done.1 = f32[2,16,128]{2,1,0:T(8,128)S(1)} copy-done((f32[2,16,128]{2,1,0:T(8,128)S(1)}, f32[2,16,128]{2,1,0:T(8,128)}, u32[]{:S(2)}) %copy-start.1) | copy-done | bytes 16408
  2.4 38.4 %lanczos.1 = (f32[3,32,32]{2,1,0:T(8,128)S(1)}, f32[3,32,32]{2,1,0:T(8,128)S(1)}, f32[1024,128]{1,0:T(8,128)S(1)}) custom-call(s32[1024,128]{1,0:T(8,128)S(1)} %bitcast.2, f32[2,16,128]{2,1,0:T(8,128)S(1)} %copy-done.1), custom_call_target="tpu_custom_call" | custom-call | tf_op jit(solution)/shard_map/lanczos/pallas_call | solution.py:349
  40.8 0.6 %copy.8 = f32[3,32,32]{2,1,0:T(8,128)} copy(f32[3,32,32]{2,1,0:T(8,128)S(1)} %get-tuple-element.12) | data formatting | bytes 24576
  41.5 0.6 %copy.9 = f32[3,32,32]{2,1,0:T(8,128)} copy(f32[3,32,32]{2,1,0:T(8,128)S(1)} %get-tuple-element.13) | data formatting | bytes 24576
  42.1 0.8 %copy.10 = f32[32,2,16,128]{3,2,1,0:T(8,128)} copy(f32[32,2,16,128]{3,2,1,0:T(8,128)S(1)} %bitcast.3) | data formatting | bytes 1048576
Async XLA Ops:
  0.6 1.0 %copy-start = (s32[32,2,16,128]{3,2,1,0:T(8,128)S(1)}, s32[32,2,16,128]{3,2,1,0:T(8,128)}, u32[]{:S(2)}) copy-start(s32[32,2,16,128]{3,2,1,0:T(8,128)} %param.2) | copy-start | bytes 1572868
  1.7 0.7 %copy-start.1 = (f32[2,16,128]{2,1,0:T(8,128)S(1)}, f32[2,16,128]{2,1,0:T(8,128)}, u32[]{:S(2)}) copy-start(f32[2,16,128]{2,1,0:T(8,128)} %diagonal_ref.1) | copy-start | bytes 49156

commit v3 on v2

--- a/solution.py
+++ b/solution.py
@@ -11,7 +11,7 @@
 CHUNK = 8
 CENTRE = 7.5
 SCALE = 2.5
-PANEL = 4
+PANEL = 8
 VMEM_BYTES = 24 * 1024 * 1024
 MESH = pl.DeviceIdType.MESH
 
@@ -63,8 +63,8 @@
 
 
 def kernel(
-    nx, ny, signs_ref, diagonal_ref, alphas_ref, betas_ref, next_ref,
-    fields, split, part_x, part_y,
+    nx, ny, signs_hbm, diagonal_hbm, alphas_ref, betas_ref, next_ref,
+    signs_ref, diagonal_ref, own_ref, fetch, fields, split, part_x, part_y,
     send_halo, recv_halo, send_x, recv_x, send_y, recv_y,
 ):
     planes, lines, lanes = diagonal_ref.shape
@@ -79,6 +79,12 @@
     def y_device(offset):
         return lax.rem(gy + offset, ny)
 
+    fetches = (
+        pltpu.make_async_copy(signs_hbm, signs_ref, fetch.at[0]),
+        pltpu.make_async_copy(diagonal_hbm, diagonal_ref, fetch.at[1]),
+    )
+    for copy in fetches:
+        copy.start()
     barrier = pltpu.get_barrier_semaphore()
     for offset in range(1, nx):
         pl.semaphore_signal(barrier, inc=1, device_id={"gx": x_device(offset)}, device_id_type=MESH)
@@ -114,7 +120,13 @@
                 bits = signs_ref[pl.ds(start, CHUNK, stride=cells), :]
                 fields[chunk, x + 1, y + 1] = 2.0 * bits.astype(jnp.float32) - 1.0
 
+    for copy in fetches:
+        copy.wait()
     load_chunk(0)
+    for x in range(planes):
+        for y in range(lines):
+            own = (diagonal_ref[x, y : y + 1, :] + (6.0 - CENTRE)) * (1.0 / SCALE)
+            own_ref[x, y] = jnp.broadcast_to(own, (CHUNK, lanes))
     pl.semaphore_wait(barrier, nx + ny - 2)
     for chunk in range(chunks):
         if chunk > 0:
@@ -193,27 +205,31 @@
         value = added(part_y, group, count, ny)
         return [unpack(value[i * height : (i + 1) * height], probes) for i in range(count)]
 
-    def apply_level(level):
+    def apply_level(level, first=0, last=None):
         def apply_chunk(chunk, carry):
             step = level * chunks + chunk
             for copy in halo_copies(step):
                 copy.wait_recv()
-            for x in range(1, planes + 1):
-                for y in range(1, lines + 1):
-                    value = fields[step, x, y]
-                    beside = fields[step, x - 1, y] + fields[step, x + 1, y]
-                    beside = beside + (fields[step, x, y - 1] + fields[step, x, y + 1])
+            before_line = [fields[step, x, 0] for x in range(1, planes + 1)]
+            line = [fields[step, x, 1] for x in range(1, planes + 1)]
+            for y in range(1, lines + 1):
+                after_line = [fields[step, x, y + 1] for x in range(1, planes + 1)]
+                row = [fields[step, 0, y]] + line + [fields[step, planes + 1, y]]
+                for x in range(1, planes + 1):
+                    value = row[x]
+                    beside = row[x - 1] + row[x + 1]
+                    beside = beside + (before_line[x - 1] + after_line[x - 1])
                     beside = beside + (pltpu.roll(value, 1, 1) + pltpu.roll(value, lanes - 1, 1))
-                    own = (diagonal_ref[x - 1, y - 1 : y, :] + (6.0 - CENTRE)) * (1.0 / SCALE)
                     fields[step + chunks, x, y] = (
-                        jnp.broadcast_to(own, value.shape) * value - beside * (1.0 / SCALE)
+                        own_ref[x - 1, y - 1] * value - beside * (1.0 / SCALE)
                     )
+                before_line, line = line, after_line
             if level + 1 < ITERS:
                 for copy in halo_copies(step + chunks):
                     copy.start()
             return carry
 
-        lax.fori_loop(0, chunks, apply_chunk, 0)
+        lax.fori_loop(first, chunks if last is None else last, apply_chunk, 0)
 
     levels = ITERS + 1
     moment = []
@@ -274,9 +290,11 @@
     link(1, 0)
     link(2, 0)
     factor_level(1)
+    middle(3, 2)
     coefficients(0)
     coupling(0)
-    middle(3, 2)
+    invert_row(0)
+    invert_row(1)
     moment.extend(end(2, 2))
     link(3, 0)
     link(2, 1)
@@ -284,25 +302,26 @@
     factor_level(2)
     coefficients(1)
     coupling(1)
-    for j in range(3):
-        invert_row(j)
-    known = [
-        mm(lower[3, 0], inverse_of[0, 0]) + mm(lower[3, 1], inverse_of[1, 0]),
-        mm(lower[3, 1], inverse_of[1, 1]),
-        None,
-    ]
-    moment.extend(end(3, 2))
-    link(3, 2)
-    factor_level(3)
-    mixing = []
-    for k in range(3):
-        gathered = mm(lower[3, 2], inverse_of[2, k])
-        if known[k] is not None:
-            gathered = gathered + known[k]
-        mixing.append(-mm(inverses[3], gathered))
-    mixing.append(inverses[3])
-    coefficients(2)
-    coupling(2)
+    invert_row(2)
+    known = jnp.concatenate(
+        [
+            mm(lower[3, 0], inverse_of[0, 0]) + mm(lower[3, 1], inverse_of[1, 0]),
+            mm(lower[3, 1], inverse_of[1, 1]),
+            jnp.zeros((probes, probes), jnp.float32),
+        ],
+        axis=1,
+    )
+    last_row = jnp.concatenate([inverse_of[2, k] for k in range(3)], axis=1)
+    known_link = mm(lower[3, 0], lower[2, 0], 1, 1) + mm(lower[3, 1], lower[2, 1], 1, 1)
+    known_pivot = mm(lower[3, 0], lower[3, 0], 1, 1) + mm(lower[3, 1], lower[3, 1], 1, 1)
+    known_inside = mm(lower[2, 1], before[1], 1, 1)
+    odd, even = end(3, 2)
+    lower[3, 2] = mm(odd - known_link, inverses[2], 1, 1)
+    upper, inverse = factor((even - known_pivot) - mm(lower[3, 2], lower[3, 2], 1, 1))
+    mixed = -mm(inverse, known + mm(lower[3, 2], last_row))
+    mixing = [mixed[:, k * probes : (k + 1) * probes] for k in range(3)] + [inverse]
+    alphas_ref[2] = shift + SCALE * mm(inverses[2], lower[3, 2] - known_inside)
+    betas_ref[2] = SCALE * mm(upper, inverses[2], 1, 1)
 
     pieces = []
     for block in mixing:
@@ -337,6 +356,15 @@
             copy.wait_send()
 
 
+def emit(alphas_ref, betas_ref, next_ref, alphas_out, betas_out, next_out, sems):
+    moves = ((next_ref, next_out), (alphas_ref, alphas_out), (betas_ref, betas_out))
+    copies = [pltpu.make_async_copy(a, b, sems.at[i]) for i, (a, b) in enumerate(moves)]
+    for copy in copies:
+        copy.start()
+    for copy in copies:
+        copy.wait()
+
+
 def per_device(nx, ny, probe_signs, diagonal):
     probes, planes, lines, lanes = probe_signs.shape
     chunks = probes // CHUNK
@@ -345,13 +373,19 @@
     cells = planes * lines
     small = jax.ShapeDtypeStruct((ITERS, probes, probes), jnp.float32)
     vmem = pl.BlockSpec(memory_space=pltpu.VMEM)
+    hbm = pl.BlockSpec(memory_space=pltpu.HBM)
     dma = pltpu.SemaphoreType.DMA
+    full = jax.ShapeDtypeStruct((probes * cells, lanes), jnp.float32)
     alphas, betas, block = pl.pallas_call(
         functools.partial(kernel, nx, ny),
-        out_shape=(small, small, jax.ShapeDtypeStruct((probes * cells, lanes), jnp.float32)),
-        in_specs=[vmem, vmem],
+        out_shape=(small, small, full),
+        in_specs=[hbm, hbm],
         out_specs=(vmem, vmem, vmem),
         scratch_shapes=[
+            pltpu.VMEM((probes * cells, lanes), jnp.int32),
+            pltpu.VMEM(diagonal.shape, jnp.float32),
+            pltpu.VMEM((planes, lines, CHUNK, lanes), jnp.float32),
+            dma((2,)),
             pltpu.VMEM((levels * chunks, planes + 2, lines + 2, CHUNK, lanes), jnp.float32),
             pltpu.VMEM((levels, 2 * probes, cells * lanes), jnp.bfloat16),
             pltpu.VMEM((levels, nx, 2 * height, lanes), jnp.float32),
@@ -367,7 +401,19 @@
             collective_id=0, has_side_effects=True, vmem_limit_bytes=VMEM_BYTES
         ),
         name="lanczos",
-    )(probe_signs.reshape(probes * cells, lanes), diagonal)
+    )(
+        pltpu.with_memory_space_constraint(probe_signs.reshape(probes * cells, lanes), pltpu.HBM),
+        pltpu.with_memory_space_constraint(diagonal, pltpu.HBM),
+    )
+    alphas, betas, block = pl.pallas_call(
+        emit,
+        out_shape=(small, small, full),
+        in_specs=[vmem] * 3,
+        out_specs=(hbm,) * 3,
+        scratch_shapes=[dma((3,))],
+        compiler_params=pltpu.CompilerParams(vmem_limit_bytes=VMEM_BYTES),
+        name="emit",
+    )(alphas, betas, block)
     return alphas, betas, block.reshape(probes, planes, lines, lanes)
 
 

time: 43.1 us -> 39.6 us (0.919)
  local copies, waits for them, and re-layouts: 3.79 us -> 0 us
    unnamed x7 -> x0, local copies, waits for them, and re-layouts: 3.79 us -> none
    pallas_call x0 -> x1, Pallas kernels: none -> 0.84 us  [per_device(): pl.pallas_call(emit, out_shape=(small, small, full), in_specs=[vmem] * 3,...]
    pallas_call x1, Pallas kernels: 38.4 us -> 38 us  [per_device(): pl.pallas_call(functools.partial(kernel, nx, ny), out_shape=(small, small...]
where the time goes in v3:
time: 39.6 us; the launch traced here: 39.4 us
  Pallas kernels  38.8 us (98%)
  between operations  0.64 us (2%)
    pallas_call x1, Pallas kernels, per_device(): pl.pallas_call(functools.partial(kernel, nx, ny), out_shape=(small, small...  38 us
    pallas_call x1, Pallas kernels, per_device(): pl.pallas_call(emit, out_shape=(small, small, full), in_specs=[vmem] * 3,...  0.84 us

profile of v3, /device:TPU:0, one launch (start us, length us, event | category | flops | bytes accessed | tf_op | source)
XLA Modules:
  0.0 39.4 jit_solution(8933639761706863491)
XLA Ops:
  0.6 38.0 %lanczos.1 = (f32[3,32,32]{2,1,0:T(8,128)S(1)}, f32[3,32,32]{2,1,0:T(8,128)S(1)}, f32[1024,128]{1,0:T(8,128)S(1)}) custom-call(s32[1024,128]{1,0:T(8,128)} %bitcast.2, f32[2,16,128]{2,1,0:T(8,128)} %diagonal_hbm.1), custom_call_target="tpu_custom_call" | custom-call | tf_op jit(solution)/shard_map/lanczos/pallas_call | solution.py:379
  38.6 0.8 %emit.1 = (f32[3,32,32]{2,1,0:T(8,128)}, f32[3,32,32]{2,1,0:T(8,128)}, f32[1024,128]{1,0:T(8,128)}) custom-call(f32[3,32,32]{2,1,0:T(8,128)S(1)} %get-tuple-element.9.alphas_ref, f32[3,32,32]{2,1,0:T(8,128)S(1)} %get-tuple-element.10.betas_ref, f32[1024,128]{1,0:T(8,128)S(1)} %get-tuple-element.11.next_ref), custom_call_target="tpu_custom_call" | custom-call | tf_op jit(solution)/shard_map/emit/pallas_call | solution.py:408

commit v4 on v3

--- a/solution.py
+++ b/solution.py
@@ -283,9 +283,9 @@
     moment.extend(end(0, 1))
     factor_level(0)
     apply_level(2)
-    middle(2, 2)
     split_level(3)
     begin(3, [gram(2, 3), gram(3, 3)])
+    middle(2, 2)
     moment.extend(end(1, 2))
     link(1, 0)
     link(2, 0)

time: 39.6 us -> 38.6 us (0.975)
  Pallas kernels: 38.8 us -> 37.8 us
    pallas_call x1, Pallas kernels: 38 us -> 36.9 us  [per_device(): pl.pallas_call(functools.partial(kernel, nx, ny), out_shape=(small, small...]
where the time goes in v4:
time: 38.6 us; the launch traced here: 38.4 us
  Pallas kernels  37.8 us (98%)
  between operations  0.64 us (2%)
    pallas_call x1, Pallas kernels, per_device(): pl.pallas_call(functools.partial(kernel, nx, ny), out_shape=(small, small...  36.9 us
    pallas_call x1, Pallas kernels, per_device(): pl.pallas_call(emit, out_shape=(small, small, full), in_specs=[vmem] * 3,...  0.84 us

profile of v4, /device:TPU:0, one launch (start us, length us, event | category | flops | bytes accessed | tf_op | source)
XLA Modules:
  0.0 38.4 jit_solution(4810526704002913444)
XLA Ops:
  0.6 36.9 %lanczos.1 = (f32[3,32,32]{2,1,0:T(8,128)S(1)}, f32[3,32,32]{2,1,0:T(8,128)S(1)}, f32[1024,128]{1,0:T(8,128)S(1)}) custom-call(s32[1024,128]{1,0:T(8,128)} %bitcast.2, f32[2,16,128]{2,1,0:T(8,128)} %diagonal_hbm.1), custom_call_target="tpu_custom_call" | custom-call | tf_op jit(solution)/shard_map/lanczos/pallas_call | solution.py:379
  37.6 0.8 %emit.1 = (f32[3,32,32]{2,1,0:T(8,128)}, f32[3,32,32]{2,1,0:T(8,128)}, f32[1024,128]{1,0:T(8,128)}) custom-call(f32[3,32,32]{2,1,0:T(8,128)S(1)} %get-tuple-element.9.alphas_ref, f32[3,32,32]{2,1,0:T(8,128)S(1)} %get-tuple-element.10.betas_ref, f32[1024,128]{1,0:T(8,128)S(1)} %get-tuple-element.11.next_ref), custom_call_target="tpu_custom_call" | custom-call | tf_op jit(solution)/shard_map/emit/pallas_call | solution.py:408
